TPU v7x, 32 devices: a whole 2x2x4 slice. The times are simulated.
32 devices in a mesh: pairs: 2 (over x), band: 16 (over z, y, core).
Axes of the slice: x: 2, y: 2, z: 4, core: 2. Of those that a mesh axis runs over, the one named last changes fastest.
Arguments:
- query_tiles: bfloat16 [512, 256, 128], P(('pairs', 'band')), parts along dimension 0, may hold values from -52 to 52
- target: bfloat16 [512, 256, 128], P(('pairs', 'band')), parts along dimension 0, may hold values from -6 to 6
- tile_home: int32 [512], P('pairs'), parts along dimension 0, may hold values from 0 to 255, as said below
- candidates: int32 [512, 64], P(('pairs', 'band')), parts along dimension 0, may hold values from 0 to 255, as said below
- valid_mask: int32 [512, 64], P(('pairs', 'band')), parts along dimension 0, may hold values from 0 to 1, as said below
Outputs:
- matched: bfloat16 [512, 256, 128], P(('pairs', 'band')), parts along dimension 0
There are 2 independent parts, one for each index of `pairs`. A program takes and returns all parts, laid end to end along the dimension named above; each array names one. Nothing has to cross between parts.
Inputs may be any that keep to these rules, and one draw needn't show every extreme that they name: `tile_home`: a permutation of 0 to 255; target tile ids that agree modulo 16 are stored on the same device, storage row r lying on device r // 16. Ids in a row are distinct; the candidates of one device's query tiles all lie in one run of 128 consecutive ids taken modulo 256, and its first two query tiles together name every id of that run. `valid_mask`: the first entry of every row is 1.
All inputs are finite; a program needn't handle non-finite values.
Results may differ from a plain program's by a relative error of at most 0.0034.
Values may be sent and summed in bfloat16 or wider, within the bound.
No kernel may reach another device: no remote copies, remote signals or barrier semaphores. Data moves between devices by JAX's collectives and lax.ppermute only.
A program may use at most 128 MiB of HBM per device.

v0:
```python
import math
import jax
import jax.numpy as jnp
from jax import lax
from jax.sharding import PartitionSpec as P


def attend_tile(tile_query, tile_keys, keep_mask):
    per_tile = tile_keys.shape[0] // keep_mask.shape[0]
    scores = jnp.dot(tile_query, tile_keys.T, preferred_element_type=jnp.float32) * (
        1.0 / math.sqrt(tile_query.shape[1])
    )
    allowed = jnp.repeat(keep_mask > 0, per_tile)[None, :]
    scores = jnp.where(allowed, scores, -jnp.inf)
    peak = jnp.max(scores, axis=1, keepdims=True)
    raised = jnp.exp(scores - peak)
    totals = jnp.sum(raised, axis=1, keepdims=True)
    weights = (raised / totals).astype(jnp.bfloat16)
    return jnp.dot(weights, tile_keys, preferred_element_type=jnp.float32).astype(jnp.bfloat16)


def body(query_tiles, target, tile_home, candidates, valid_mask):
    channels = target.shape[2]
    stored_rows = tile_home[candidates]
    source = lax.all_gather(target, "band", axis=0, tiled=True)

    def one_tile(packed):
        tile_query, chosen, keep_mask = packed
        stored = source[chosen].reshape(-1, channels)
        return attend_tile(tile_query, stored, keep_mask)

    return lax.map(one_tile, (query_tiles, stored_rows, valid_mask))


def solution(mesh):
    in_specs = (
        P(("pairs", "band"), None, None),
        P(("pairs", "band"), None, None),
        P("pairs"),
        P(("pairs", "band"), None),
        P(("pairs", "band"), None),
    )
    out_specs = P(("pairs", "band"), None, None)
    return jax.shard_map(body, mesh=mesh, in_specs=in_specs, out_specs=out_specs, check_vma=False)
```

profile of v0, /device:TPU:0, one launch (start us, length us, event | category | flops | bytes accessed | tf_op | source)
XLA Modules:
  0.0 721.8 jit_solution(7972578319023650568)
XLA Ops:
  15.0 123.7 %all-gather.2.cloned.1.call-done = bf16[256,256,128]{2,1,0:T(8,128)(2,1)} async-done(((bf16[16,256,128]{2,1,0:T(8,128)(2,1)}), bf16[256,256,128]{2,1,0:T(8,128)(2,1)}) %all-gather.2.cloned.1.call-update) | async-done | bytes 16777232 | tf_op jit(solution)/shard_map/all_gather | solution.py:25
  138.7 575.3 %while.10 = (s32[]{:T(128)}, bf16[16,256,128]{2,1,0:T(8,128)(2,1)S(1)}, s32[16,64]{1,0:T(8,128)}, bf16[16,256,128]{2,1,0:T(8,128)(2,1)}, s32[16,64]{1,0:T(8,128)S(1)}, /*index=5*/bf16[256,256,128]{2,1,0:T(8,128)(2,1)}, s32[]{:T(128)}) while((s32[]{:T(128)}, bf16[16,256,128]{2,1,0:T(8,128)(2,1)S(1)}, s32[16,64]{1,0:T(8,128)}, ...), condition=%wide.region_3.4_spmd, body=%wide.region_0.3_spmd.sunk | while | flops 2181071616 | bytes 84093936 | solution.py:32
  148.4 10.4 %fusion.23 = (f32[256]{0:T(256)S(1)}, f32[256,16384]{1,0:T(8,128)}) fusion(bf16[16384,128]{1,0:T(8,128)(2,1)} %bitcast.38, bf16[16,256,128]{2,1,0:T(8,128)(2,1)} %get-tuple-element.110, s32[]{:T(128)} %get-tuple-element.100, pred[16384]{0:T(1024)(128)(4,1)S(1)} %broadcast_in_dim.37), kind=kOutput, calls=%fused_computation.23.clone.1 | convolution fusion | flops 1086324480 | bytes 21054976 | tf_op jit(solution)/shard_map/while/body/eval_jaxpr/dot_general | solution.py:10
  174.7 8.9 %gather_fusion = bf16[64,256,128]{2,1,0:T(8,128)(2,1)} fusion(bf16[256,256,128]{2,1,0:T(8,128)(2,1)} %get-tuple-element.112, s32[1024]{0:T(1024)S(1)} %pad_clamp_fusion.2), kind=kCustom, calls=%fused_computation.clone.1 | custom fusion | bytes 8388864 | tf_op jit(solution)/shard_map/while/body/eval_jaxpr/gather | solution.py:29
  184.4 10.4 %fusion.23 = (f32[256]{0:T(256)S(1)}, f32[256,16384]{1,0:T(8,128)}) fusion(bf16[16384,128]{1,0:T(8,128)(2,1)} %bitcast.38, bf16[16,256,128]{2,1,0:T(8,128)(2,1)} %get-tuple-element.110, s32[]{:T(128)} %get-tuple-element.100, pred[16384]{0:T(1024)(128)(4,1)S(1)} %broadcast_in_dim.37), kind=kOutput, calls=%fused_computation.23.clone.1 | convolution fusion | flops 1086324480 | bytes 21054976 | tf_op jit(solution)/shard_map/while/body/eval_jaxpr/dot_general | solution.py:10
  210.6 8.9 %gather_fusion = bf16[64,256,128]{2,1,0:T(8,128)(2,1)} fusion(bf16[256,256,128]{2,1,0:T(8,128)(2,1)} %get-tuple-element.112, s32[1024]{0:T(1024)S(1)} %pad_clamp_fusion.2), kind=kCustom, calls=%fused_computation.clone.1 | custom fusion | bytes 8388864 | tf_op jit(solution)/shard_map/while/body/eval_jaxpr/gather | solution.py:29
  220.3 10.4 %fusion.23 = (f32[256]{0:T(256)S(1)}, f32[256,16384]{1,0:T(8,128)}) fusion(bf16[16384,128]{1,0:T(8,128)(2,1)} %bitcast.38, bf16[16,256,128]{2,1,0:T(8,128)(2,1)} %get-tuple-element.110, s32[]{:T(128)} %get-tuple-element.100, pred[16384]{0:T(1024)(128)(4,1)S(1)} %broadcast_in_dim.37), kind=kOutput, calls=%fused_computation.23.clone.1 | convolution fusion | flops 1086324480 | bytes 21054976 | tf_op jit(solution)/shard_map/while/body/eval_jaxpr/dot_general | solution.py:10
  256.3 10.4 %fusion.23 = (f32[256]{0:T(256)S(1)}, f32[256,16384]{1,0:T(8,128)}) fusion(bf16[16384,128]{1,0:T(8,128)(2,1)} %bitcast.38, bf16[16,256,128]{2,1,0:T(8,128)(2,1)} %get-tuple-element.110, s32[]{:T(128)} %get-tuple-element.100, pred[16384]{0:T(1024)(128)(4,1)S(1)} %broadcast_in_dim.37), kind=kOutput, calls=%fused_computation.23.clone.1 | convolution fusion | flops 1086324480 | bytes 21054976 | tf_op jit(solution)/shard_map/while/body/eval_jaxpr/dot_general | solution.py:10
  282.5 8.9 %gather_fusion = bf16[64,256,128]{2,1,0:T(8,128)(2,1)} fusion(bf16[256,256,128]{2,1,0:T(8,128)(2,1)} %get-tuple-element.112, s32[1024]{0:T(1024)S(1)} %pad_clamp_fusion.2), kind=kCustom, calls=%fused_computation.clone.1 | custom fusion | bytes 8388864 | tf_op jit(solution)/shard_map/while/body/eval_jaxpr/gather | solution.py:29
  292.2 10.4 %fusion.23 = (f32[256]{0:T(256)S(1)}, f32[256,16384]{1,0:T(8,128)}) fusion(bf16[16384,128]{1,0:T(8,128)(2,1)} %bitcast.38, bf16[16,256,128]{2,1,0:T(8,128)(2,1)} %get-tuple-element.110, s32[]{:T(128)} %get-tuple-element.100, pred[16384]{0:T(1024)(128)(4,1)S(1)} %broadcast_in_dim.37), kind=kOutput, calls=%fused_computation.23.clone.1 | convolution fusion | flops 1086324480 | bytes 21054976 | tf_op jit(solution)/shard_map/while/body/eval_jaxpr/dot_general | solution.py:10
  328.2 10.4 %fusion.23 = (f32[256]{0:T(256)S(1)}, f32[256,16384]{1,0:T(8,128)}) fusion(bf16[16384,128]{1,0:T(8,128)(2,1)} %bitcast.38, bf16[16,256,128]{2,1,0:T(8,128)(2,1)} %get-tuple-element.110, s32[]{:T(128)} %get-tuple-element.100, pred[16384]{0:T(1024)(128)(4,1)S(1)} %broadcast_in_dim.37), kind=kOutput, calls=%fused_computation.23.clone.1 | convolution fusion | flops 1086324480 | bytes 21054976 | tf_op jit(solution)/shard_map/while/body/eval_jaxpr/dot_general | solution.py:10
  364.2 10.4 %fusion.23 = (f32[256]{0:T(256)S(1)}, f32[256,16384]{1,0:T(8,128)}) fusion(bf16[16384,128]{1,0:T(8,128)(2,1)} %bitcast.38, bf16[16,256,128]{2,1,0:T(8,128)(2,1)} %get-tuple-element.110, s32[]{:T(128)} %get-tuple-element.100, pred[16384]{0:T(1024)(128)(4,1)S(1)} %broadcast_in_dim.37), kind=kOutput, calls=%fused_computation.23.clone.1 | convolution fusion | flops 1086324480 | bytes 21054976 | tf_op jit(solution)/shard_map/while/body/eval_jaxpr/dot_general | solution.py:10
  400.1 10.4 %fusion.23 = (f32[256]{0:T(256)S(1)}, f32[256,16384]{1,0:T(8,128)}) fusion(bf16[16384,128]{1,0:T(8,128)(2,1)} %bitcast.38, bf16[16,256,128]{2,1,0:T(8,128)(2,1)} %get-tuple-element.110, s32[]{:T(128)} %get-tuple-element.100, pred[16384]{0:T(1024)(128)(4,1)S(1)} %broadcast_in_dim.37), kind=kOutput, calls=%fused_computation.23.clone.1 | convolution fusion | flops 1086324480 | bytes 21054976 | tf_op jit(solution)/shard_map/while/body/eval_jaxpr/dot_general | solution.py:10
  426.4 8.9 %gather_fusion = bf16[64,256,128]{2,1,0:T(8,128)(2,1)} fusion(bf16[256,256,128]{2,1,0:T(8,128)(2,1)} %get-tuple-element.112, s32[1024]{0:T(1024)S(1)} %pad_clamp_fusion.2), kind=kCustom, calls=%fused_computation.clone.1 | custom fusion | bytes 8388864 | tf_op jit(solution)/shard_map/while/body/eval_jaxpr/gather | solution.py:29
  436.1 10.4 %fusion.23 = (f32[256]{0:T(256)S(1)}, f32[256,16384]{1,0:T(8,128)}) fusion(bf16[16384,128]{1,0:T(8,128)(2,1)} %bitcast.38, bf16[16,256,128]{2,1,0:T(8,128)(2,1)} %get-tuple-element.110, s32[]{:T(128)} %get-tuple-element.100, pred[16384]{0:T(1024)(128)(4,1)S(1)} %broadcast_in_dim.37), kind=kOutput, calls=%fused_computation.23.clone.1 | convolution fusion | flops 1086324480 | bytes 21054976 | tf_op jit(solution)/shard_map/while/body/eval_jaxpr/dot_general | solution.py:10
  472.0 10.4 %fusion.23 = (f32[256]{0:T(256)S(1)}, f32[256,16384]{1,0:T(8,128)}) fusion(bf16[16384,128]{1,0:T(8,128)(2,1)} %bitcast.38, bf16[16,256,128]{2,1,0:T(8,128)(2,1)} %get-tuple-element.110, s32[]{:T(128)} %get-tuple-element.100, pred[16384]{0:T(1024)(128)(4,1)S(1)} %broadcast_in_dim.37), kind=kOutput, calls=%fused_computation.23.clone.1 | convolution fusion | flops 1086324480 | bytes 21054976 | tf_op jit(solution)/shard_map/while/body/eval_jaxpr/dot_general | solution.py:10
  508.0 10.4 %fusion.23 = (f32[256]{0:T(256)S(1)}, f32[256,16384]{1,0:T(8,128)}) fusion(bf16[16384,128]{1,0:T(8,128)(2,1)} %bitcast.38, bf16[16,256,128]{2,1,0:T(8,128)(2,1)} %get-tuple-element.110, s32[]{:T(128)} %get-tuple-element.100, pred[16384]{0:T(1024)(128)(4,1)S(1)} %broadcast_in_dim.37), kind=kOutput, calls=%fused_computation.23.clone.1 | convolution fusion | flops 1086324480 | bytes 21054976 | tf_op jit(solution)/shard_map/while/body/eval_jaxpr/dot_general | solution.py:10
  534.2 8.9 %gather_fusion = bf16[64,256,128]{2,1,0:T(8,128)(2,1)} fusion(bf16[256,256,128]{2,1,0:T(8,128)(2,1)} %get-tuple-element.112, s32[1024]{0:T(1024)S(1)} %pad_clamp_fusion.2), kind=kCustom, calls=%fused_computation.clone.1 | custom fusion | bytes 8388864 | tf_op jit(solution)/shard_map/while/body/eval_jaxpr/gather | solution.py:29
  544.0 10.4 %fusion.23 = (f32[256]{0:T(256)S(1)}, f32[256,16384]{1,0:T(8,128)}) fusion(bf16[16384,128]{1,0:T(8,128)(2,1)} %bitcast.38, bf16[16,256,128]{2,1,0:T(8,128)(2,1)} %get-tuple-element.110, s32[]{:T(128)} %get-tuple-element.100, pred[16384]{0:T(1024)(128)(4,1)S(1)} %broadcast_in_dim.37), kind=kOutput, calls=%fused_computation.23.clone.1 | convolution fusion | flops 1086324480 | bytes 21054976 | tf_op jit(solution)/shard_map/while/body/eval_jaxpr/dot_general | solution.py:10
  579.9 10.4 %fusion.23 = (f32[256]{0:T(256)S(1)}, f32[256,16384]{1,0:T(8,128)}) fusion(bf16[16384,128]{1,0:T(8,128)(2,1)} %bitcast.38, bf16[16,256,128]{2,1,0:T(8,128)(2,1)} %get-tuple-element.110, s32[]{:T(128)} %get-tuple-element.100, pred[16384]{0:T(1024)(128)(4,1)S(1)} %broadcast_in_dim.37), kind=kOutput, calls=%fused_computation.23.clone.1 | convolution fusion | flops 1086324480 | bytes 21054976 | tf_op jit(solution)/shard_map/while/body/eval_jaxpr/dot_general | solution.py:10
  615.9 10.4 %fusion.23 = (f32[256]{0:T(256)S(1)}, f32[256,16384]{1,0:T(8,128)}) fusion(bf16[16384,128]{1,0:T(8,128)(2,1)} %bitcast.38, bf16[16,256,128]{2,1,0:T(8,128)(2,1)} %get-tuple-element.110, s32[]{:T(128)} %get-tuple-element.100, pred[16384]{0:T(1024)(128)(4,1)S(1)} %broadcast_in_dim.37), kind=kOutput, calls=%fused_computation.23.clone.1 | convolution fusion | flops 1086324480 | bytes 21054976 | tf_op jit(solution)/shard_map/while/body/eval_jaxpr/dot_general | solution.py:10
  651.8 10.4 %fusion.23 = (f32[256]{0:T(256)S(1)}, f32[256,16384]{1,0:T(8,128)}) fusion(bf16[16384,128]{1,0:T(8,128)(2,1)} %bitcast.38, bf16[16,256,128]{2,1,0:T(8,128)(2,1)} %get-tuple-element.110, s32[]{:T(128)} %get-tuple-element.100, pred[16384]{0:T(1024)(128)(4,1)S(1)} %broadcast_in_dim.37), kind=kOutput, calls=%fused_computation.23.clone.1 | convolution fusion | flops 1086324480 | bytes 21054976 | tf_op jit(solution)/shard_map/while/body/eval_jaxpr/dot_general | solution.py:10
  678.1 8.9 %gather_fusion = bf16[64,256,128]{2,1,0:T(8,128)(2,1)} fusion(bf16[256,256,128]{2,1,0:T(8,128)(2,1)} %get-tuple-element.112, s32[1024]{0:T(1024)S(1)} %pad_clamp_fusion.2), kind=kCustom, calls=%fused_computation.clone.1 | custom fusion | bytes 8388864 | tf_op jit(solution)/shard_map/while/body/eval_jaxpr/gather | solution.py:29
  687.8 10.4 %fusion.23 = (f32[256]{0:T(256)S(1)}, f32[256,16384]{1,0:T(8,128)}) fusion(bf16[16384,128]{1,0:T(8,128)(2,1)} %bitcast.38, bf16[16,256,128]{2,1,0:T(8,128)(2,1)} %get-tuple-element.110, s32[]{:T(128)} %get-tuple-element.100, pred[16384]{0:T(1024)(128)(4,1)S(1)} %broadcast_in_dim.37), kind=kOutput, calls=%fused_computation.23.clone.1 | convolution fusion | flops 1086324480 | bytes 21054976 | tf_op jit(solution)/shard_map/while/body/eval_jaxpr/dot_general | solution.py:10
  (166 shorter events, 363.3 us)
Async XLA Ops:
  6.5 1.5 copy-start
  6.5 132.1 %all-gather.2.cloned.1.call-start = ((), (), s32[]{:S(2)}) async-start(), calls=%async_computation | async-start | bytes 17825792 | tf_op jit(solution)/shard_map/all_gather | solution.py:25
  148.4 18.6 %copy-start.1 = (bf16[64,256,128]{2,1,0:T(8,128)(2,1)S(1)}, bf16[64,256,128]{2,1,0:T(8,128)(2,1)}, u32[]{:S(2)}) copy-start(bf16[64,256,128]{2,1,0:T(8,128)(2,1)} %gather_fusion) | copy-start | bytes 12582916 | tf_op jit(solution)/shard_map/while
  184.4 18.6 %copy-start.1 = (bf16[64,256,128]{2,1,0:T(8,128)(2,1)S(1)}, bf16[64,256,128]{2,1,0:T(8,128)(2,1)}, u32[]{:S(2)}) copy-start(bf16[64,256,128]{2,1,0:T(8,128)(2,1)} %gather_fusion) | copy-start | bytes 12582916 | tf_op jit(solution)/shard_map/while
  220.3 18.6 %copy-start.1 = (bf16[64,256,128]{2,1,0:T(8,128)(2,1)S(1)}, bf16[64,256,128]{2,1,0:T(8,128)(2,1)}, u32[]{:S(2)}) copy-start(bf16[64,256,128]{2,1,0:T(8,128)(2,1)} %gather_fusion) | copy-start | bytes 12582916 | tf_op jit(solution)/shard_map/while
  256.3 18.6 %copy-start.1 = (bf16[64,256,128]{2,1,0:T(8,128)(2,1)S(1)}, bf16[64,256,128]{2,1,0:T(8,128)(2,1)}, u32[]{:S(2)}) copy-start(bf16[64,256,128]{2,1,0:T(8,128)(2,1)} %gather_fusion) | copy-start | bytes 12582916 | tf_op jit(solution)/shard_map/while
  292.2 18.6 %copy-start.1 = (bf16[64,256,128]{2,1,0:T(8,128)(2,1)S(1)}, bf16[64,256,128]{2,1,0:T(8,128)(2,1)}, u32[]{:S(2)}) copy-start(bf16[64,256,128]{2,1,0:T(8,128)(2,1)} %gather_fusion) | copy-start | bytes 12582916 | tf_op jit(solution)/shard_map/while
  328.2 18.6 %copy-start.1 = (bf16[64,256,128]{2,1,0:T(8,128)(2,1)S(1)}, bf16[64,256,128]{2,1,0:T(8,128)(2,1)}, u32[]{:S(2)}) copy-start(bf16[64,256,128]{2,1,0:T(8,128)(2,1)} %gather_fusion) | copy-start | bytes 12582916 | tf_op jit(solution)/shard_map/while
  364.2 18.6 %copy-start.1 = (bf16[64,256,128]{2,1,0:T(8,128)(2,1)S(1)}, bf16[64,256,128]{2,1,0:T(8,128)(2,1)}, u32[]{:S(2)}) copy-start(bf16[64,256,128]{2,1,0:T(8,128)(2,1)} %gather_fusion) | copy-start | bytes 12582916 | tf_op jit(solution)/shard_map/while
  400.1 18.6 %copy-start.1 = (bf16[64,256,128]{2,1,0:T(8,128)(2,1)S(1)}, bf16[64,256,128]{2,1,0:T(8,128)(2,1)}, u32[]{:S(2)}) copy-start(bf16[64,256,128]{2,1,0:T(8,128)(2,1)} %gather_fusion) | copy-start | bytes 12582916 | tf_op jit(solution)/shard_map/while
  436.1 18.6 %copy-start.1 = (bf16[64,256,128]{2,1,0:T(8,128)(2,1)S(1)}, bf16[64,256,128]{2,1,0:T(8,128)(2,1)}, u32[]{:S(2)}) copy-start(bf16[64,256,128]{2,1,0:T(8,128)(2,1)} %gather_fusion) | copy-start | bytes 12582916 | tf_op jit(solution)/shard_map/while
  472.0 18.6 %copy-start.1 = (bf16[64,256,128]{2,1,0:T(8,128)(2,1)S(1)}, bf16[64,256,128]{2,1,0:T(8,128)(2,1)}, u32[]{:S(2)}) copy-start(bf16[64,256,128]{2,1,0:T(8,128)(2,1)} %gather_fusion) | copy-start | bytes 12582916 | tf_op jit(solution)/shard_map/while
  508.0 18.6 %copy-start.1 = (bf16[64,256,128]{2,1,0:T(8,128)(2,1)S(1)}, bf16[64,256,128]{2,1,0:T(8,128)(2,1)}, u32[]{:S(2)}) copy-start(bf16[64,256,128]{2,1,0:T(8,128)(2,1)} %gather_fusion) | copy-start | bytes 12582916 | tf_op jit(solution)/shard_map/while
  543.9 18.6 %copy-start.1 = (bf16[64,256,128]{2,1,0:T(8,128)(2,1)S(1)}, bf16[64,256,128]{2,1,0:T(8,128)(2,1)}, u32[]{:S(2)}) copy-start(bf16[64,256,128]{2,1,0:T(8,128)(2,1)} %gather_fusion) | copy-start | bytes 12582916 | tf_op jit(solution)/shard_map/while
  579.9 18.6 %copy-start.1 = (bf16[64,256,128]{2,1,0:T(8,128)(2,1)S(1)}, bf16[64,256,128]{2,1,0:T(8,128)(2,1)}, u32[]{:S(2)}) copy-start(bf16[64,256,128]{2,1,0:T(8,128)(2,1)} %gather_fusion) | copy-start | bytes 12582916 | tf_op jit(solution)/shard_map/while
  615.9 18.6 %copy-start.1 = (bf16[64,256,128]{2,1,0:T(8,128)(2,1)S(1)}, bf16[64,256,128]{2,1,0:T(8,128)(2,1)}, u32[]{:S(2)}) copy-start(bf16[64,256,128]{2,1,0:T(8,128)(2,1)} %gather_fusion) | copy-start | bytes 12582916 | tf_op jit(solution)/shard_map/while
  651.8 18.6 %copy-start.1 = (bf16[64,256,128]{2,1,0:T(8,128)(2,1)S(1)}, bf16[64,256,128]{2,1,0:T(8,128)(2,1)}, u32[]{:S(2)}) copy-start(bf16[64,256,128]{2,1,0:T(8,128)(2,1)} %gather_fusion) | copy-start | bytes 12582916 | tf_op jit(solution)/shard_map/while
  687.8 18.6 %copy-start.1 = (bf16[64,256,128]{2,1,0:T(8,128)(2,1)S(1)}, bf16[64,256,128]{2,1,0:T(8,128)(2,1)}, u32[]{:S(2)}) copy-start(bf16[64,256,128]{2,1,0:T(8,128)(2,1)} %gather_fusion) | copy-start | bytes 12582916 | tf_op jit(solution)/shard_map/while
  714.0 1.0 copy-start.2
Sparse Core Ops, SparseCore 0:
  9.5 129.1 all-gather.1
where the time goes:
time: 724 us; the launch traced here: 722 us
  matrix products  289 us (40%)
  local copies, waits for them, and re-layouts  152 us (21%)
  other arithmetic  142 us (20%)
  waiting for transfers between devices  124 us (17%)
  between operations  13.4 us (2%)
    dot_general x16, matrix products, attend_tile(): jnp.dot(tile_query, tile_keys.T, preferred_element_type=jnp.float32)  167 us
    gather x16, local copies, waits for them, and re-layouts, one_tile(): stored = source[chosen].reshape(-1, channels)  142 us
    reduce_sum x16, other arithmetic, attend_tile(): totals = jnp.sum(raised, axis=1, keepdims=True)  130 us
    all_gather x1, waiting for transfers between devices, body(): source = lax.all_gather(target, 'band', axis=0, tiled=True)  124 us
    dot_general x16, matrix products, attend_tile(): jnp.dot(weights, tile_keys, preferred_element_type=jnp.float32)  122 us
  transfers between devices with their start and end apart: 1, of which 1 were waited for; matrix products, arithmetic and copies ran while one was open for 1% of the time, Pallas kernels for 0%

commit v1 on v0

--- a/solution.py
+++ b/solution.py
@@ -22,7 +22,9 @@
 def body(query_tiles, target, tile_home, candidates, valid_mask):
     channels = target.shape[2]
     stored_rows = tile_home[candidates]
-    source = lax.all_gather(target, "band", axis=0, tiled=True)
+    source = jnp.concatenate(
+        lax.all_to_all(jnp.stack([target] * lax.axis_size("band")), "band", 0, 0), axis=0
+    )
 
     def one_tile(packed):
         tile_query, chosen, keep_mask = packed

time: 724 us -> 954 us (1.32)
  the two profiles are of different devices: /device:TPU:0 before, /device:TPU:13 now
where the time goes in v1:
time: 954 us; the launch traced here: 952 us
  waiting for transfers between devices  355 us (37%)
  matrix products  289 us (30%)
  local copies, waits for them, and re-layouts  159 us (17%)
  other arithmetic  142 us (15%)
    all_to_all x1, waiting for transfers between devices, body(): lax.all_to_all(jnp.stack([target] * lax.axis_size('band')), 'band', 0, 0)  355 us
    dot_general x16, matrix products, attend_tile(): jnp.dot(tile_query, tile_keys.T, preferred_element_type=jnp.float32)  167 us
    gather x16, local copies, waits for them, and re-layouts, one_tile(): stored = source[chosen].reshape(-1, channels)  142 us
    reduce_sum x16, other arithmetic, attend_tile(): totals = jnp.sum(raised, axis=1, keepdims=True)  130 us
    dot_general x16, matrix products, attend_tile(): jnp.dot(weights, tile_keys, preferred_element_type=jnp.float32)  122 us
  transfers between devices with their start and end apart: 1, of which 1 were waited for; matrix products, arithmetic and copies ran while one was open for 1% of the time, Pallas kernels for 0%

profile of v1, /device:TPU:13, one launch (start us, length us, event | category | flops | bytes accessed | tf_op | source)
XLA Modules:
  0.0 952.1 jit_solution(10594737931668483883)
XLA Ops:
  20.8 355.1 %all-to-all-done = bf16[16,16,256,128]{3,2,1,0:T(8,128)(2,1)} async-done(((bf16[16,16,256,128]{3,2,1,0:T(8,128)(2,1)}), bf16[16,16,256,128]{3,2,1,0:T(8,128)(2,1)}, u32[]{:S(2)}, u32[]{:S(2)}) %all-to-all-start) | async-done | bytes 16777248 | tf_op jit(solution)/shard_map/all_to_all | solution.py:26
  375.9 575.3 %while.10 = (s32[]{:T(128)}, bf16[16,256,128]{2,1,0:T(8,128)(2,1)S(1)}, s32[16,64]{1,0:T(8,128)}, bf16[16,256,128]{2,1,0:T(8,128)(2,1)}, s32[16,64]{1,0:T(8,128)S(1)}, /*index=5*/bf16[256,256,128]{2,1,0:T(8,128)(2,1)}, s32[]{:T(128)}) while((s32[]{:T(128)}, bf16[16,256,128]{2,1,0:T(8,128)(2,1)S(1)}, s32[16,64]{1,0:T(8,128)}, ...), condition=%wide.region_3.4_spmd, body=%wide.region_0.3_spmd.sunk | while | flops 2181071616 | bytes 84093936 | solution.py:34
  385.6 10.4 %fusion.23 = (f32[256]{0:T(256)S(1)}, f32[256,16384]{1,0:T(8,128)}) fusion(bf16[16384,128]{1,0:T(8,128)(2,1)} %bitcast.39, bf16[16,256,128]{2,1,0:T(8,128)(2,1)} %get-tuple-element.110, s32[]{:T(128)} %get-tuple-element.100, pred[16384]{0:T(1024)(128)(4,1)S(1)} %broadcast_in_dim.37), kind=kOutput, calls=%fused_computation.23.clone.1 | convolution fusion | flops 1086324480 | bytes 21054976 | tf_op jit(solution)/shard_map/while/body/eval_jaxpr/dot_general | solution.py:10
  411.8 8.9 gather_fusion
  421.6 10.4 %fusion.23 = (f32[256]{0:T(256)S(1)}, f32[256,16384]{1,0:T(8,128)}) fusion(bf16[16384,128]{1,0:T(8,128)(2,1)} %bitcast.39, bf16[16,256,128]{2,1,0:T(8,128)(2,1)} %get-tuple-element.110, s32[]{:T(128)} %get-tuple-element.100, pred[16384]{0:T(1024)(128)(4,1)S(1)} %broadcast_in_dim.37), kind=kOutput, calls=%fused_computation.23.clone.1 | convolution fusion | flops 1086324480 | bytes 21054976 | tf_op jit(solution)/shard_map/while/body/eval_jaxpr/dot_general | solution.py:10
  447.8 8.9 gather_fusion
  457.5 10.4 %fusion.23 = (f32[256]{0:T(256)S(1)}, f32[256,16384]{1,0:T(8,128)}) fusion(bf16[16384,128]{1,0:T(8,128)(2,1)} %bitcast.39, bf16[16,256,128]{2,1,0:T(8,128)(2,1)} %get-tuple-element.110, s32[]{:T(128)} %get-tuple-element.100, pred[16384]{0:T(1024)(128)(4,1)S(1)} %broadcast_in_dim.37), kind=kOutput, calls=%fused_computation.23.clone.1 | convolution fusion | flops 1086324480 | bytes 21054976 | tf_op jit(solution)/shard_map/while/body/eval_jaxpr/dot_general | solution.py:10
  483.8 8.9 gather_fusion
  493.5 10.4 %fusion.23 = (f32[256]{0:T(256)S(1)}, f32[256,16384]{1,0:T(8,128)}) fusion(bf16[16384,128]{1,0:T(8,128)(2,1)} %bitcast.39, bf16[16,256,128]{2,1,0:T(8,128)(2,1)} %get-tuple-element.110, s32[]{:T(128)} %get-tuple-element.100, pred[16384]{0:T(1024)(128)(4,1)S(1)} %broadcast_in_dim.37), kind=kOutput, calls=%fused_computation.23.clone.1 | convolution fusion | flops 1086324480 | bytes 21054976 | tf_op jit(solution)/shard_map/while/body/eval_jaxpr/dot_general | solution.py:10
  529.4 10.4 %fusion.23 = (f32[256]{0:T(256)S(1)}, f32[256,16384]{1,0:T(8,128)}) fusion(bf16[16384,128]{1,0:T(8,128)(2,1)} %bitcast.39, bf16[16,256,128]{2,1,0:T(8,128)(2,1)} %get-tuple-element.110, s32[]{:T(128)} %get-tuple-element.100, pred[16384]{0:T(1024)(128)(4,1)S(1)} %broadcast_in_dim.37), kind=kOutput, calls=%fused_computation.23.clone.1 | convolution fusion | flops 1086324480 | bytes 21054976 | tf_op jit(solution)/shard_map/while/body/eval_jaxpr/dot_general | solution.py:10
  555.7 8.9 gather_fusion
  565.4 10.4 %fusion.23 = (f32[256]{0:T(256)S(1)}, f32[256,16384]{1,0:T(8,128)}) fusion(bf16[16384,128]{1,0:T(8,128)(2,1)} %bitcast.39, bf16[16,256,128]{2,1,0:T(8,128)(2,1)} %get-tuple-element.110, s32[]{:T(128)} %get-tuple-element.100, pred[16384]{0:T(1024)(128)(4,1)S(1)} %broadcast_in_dim.37), kind=kOutput, calls=%fused_computation.23.clone.1 | convolution fusion | flops 1086324480 | bytes 21054976 | tf_op jit(solution)/shard_map/while/body/eval_jaxpr/dot_general | solution.py:10
  601.3 10.4 %fusion.23 = (f32[256]{0:T(256)S(1)}, f32[256,16384]{1,0:T(8,128)}) fusion(bf16[16384,128]{1,0:T(8,128)(2,1)} %bitcast.39, bf16[16,256,128]{2,1,0:T(8,128)(2,1)} %get-tuple-element.110, s32[]{:T(128)} %get-tuple-element.100, pred[16384]{0:T(1024)(128)(4,1)S(1)} %broadcast_in_dim.37), kind=kOutput, calls=%fused_computation.23.clone.1 | convolution fusion | flops 1086324480 | bytes 21054976 | tf_op jit(solution)/shard_map/while/body/eval_jaxpr/dot_general | solution.py:10
  637.3 10.4 %fusion.23 = (f32[256]{0:T(256)S(1)}, f32[256,16384]{1,0:T(8,128)}) fusion(bf16[16384,128]{1,0:T(8,128)(2,1)} %bitcast.39, bf16[16,256,128]{2,1,0:T(8,128)(2,1)} %get-tuple-element.110, s32[]{:T(128)} %get-tuple-element.100, pred[16384]{0:T(1024)(128)(4,1)S(1)} %broadcast_in_dim.37), kind=kOutput, calls=%fused_computation.23.clone.1 | convolution fusion | flops 1086324480 | bytes 21054976 | tf_op jit(solution)/shard_map/while/body/eval_jaxpr/dot_general | solution.py:10
  663.5 8.9 gather_fusion
  673.3 10.4 %fusion.23 = (f32[256]{0:T(256)S(1)}, f32[256,16384]{1,0:T(8,128)}) fusion(bf16[16384,128]{1,0:T(8,128)(2,1)} %bitcast.39, bf16[16,256,128]{2,1,0:T(8,128)(2,1)} %get-tuple-element.110, s32[]{:T(128)} %get-tuple-element.100, pred[16384]{0:T(1024)(128)(4,1)S(1)} %broadcast_in_dim.37), kind=kOutput, calls=%fused_computation.23.clone.1 | convolution fusion | flops 1086324480 | bytes 21054976 | tf_op jit(solution)/shard_map/while/body/eval_jaxpr/dot_general | solution.py:10
  709.2 10.4 %fusion.23 = (f32[256]{0:T(256)S(1)}, f32[256,16384]{1,0:T(8,128)}) fusion(bf16[16384,128]{1,0:T(8,128)(2,1)} %bitcast.39, bf16[16,256,128]{2,1,0:T(8,128)(2,1)} %get-tuple-element.110, s32[]{:T(128)} %get-tuple-element.100, pred[16384]{0:T(1024)(128)(4,1)S(1)} %broadcast_in_dim.37), kind=kOutput, calls=%fused_computation.23.clone.1 | convolution fusion | flops 1086324480 | bytes 21054976 | tf_op jit(solution)/shard_map/while/body/eval_jaxpr/dot_general | solution.py:10
  745.2 10.4 %fusion.23 = (f32[256]{0:T(256)S(1)}, f32[256,16384]{1,0:T(8,128)}) fusion(bf16[16384,128]{1,0:T(8,128)(2,1)} %bitcast.39, bf16[16,256,128]{2,1,0:T(8,128)(2,1)} %get-tuple-element.110, s32[]{:T(128)} %get-tuple-element.100, pred[16384]{0:T(1024)(128)(4,1)S(1)} %broadcast_in_dim.37), kind=kOutput, calls=%fused_computation.23.clone.1 | convolution fusion | flops 1086324480 | bytes 21054976 | tf_op jit(solution)/shard_map/while/body/eval_jaxpr/dot_general | solution.py:10
  781.1 10.4 %fusion.23 = (f32[256]{0:T(256)S(1)}, f32[256,16384]{1,0:T(8,128)}) fusion(bf16[16384,128]{1,0:T(8,128)(2,1)} %bitcast.39, bf16[16,256,128]{2,1,0:T(8,128)(2,1)} %get-tuple-element.110, s32[]{:T(128)} %get-tuple-element.100, pred[16384]{0:T(1024)(128)(4,1)S(1)} %broadcast_in_dim.37), kind=kOutput, calls=%fused_computation.23.clone.1 | convolution fusion | flops 1086324480 | bytes 21054976 | tf_op jit(solution)/shard_map/while/body/eval_jaxpr/dot_general | solution.py:10
  807.4 8.9 gather_fusion
  817.1 10.4 %fusion.23 = (f32[256]{0:T(256)S(1)}, f32[256,16384]{1,0:T(8,128)}) fusion(bf16[16384,128]{1,0:T(8,128)(2,1)} %bitcast.39, bf16[16,256,128]{2,1,0:T(8,128)(2,1)} %get-tuple-element.110, s32[]{:T(128)} %get-tuple-element.100, pred[16384]{0:T(1024)(128)(4,1)S(1)} %broadcast_in_dim.37), kind=kOutput, calls=%fused_computation.23.clone.1 | convolution fusion | flops 1086324480 | bytes 21054976 | tf_op jit(solution)/shard_map/while/body/eval_jaxpr/dot_general | solution.py:10
  853.0 10.4 %fusion.23 = (f32[256]{0:T(256)S(1)}, f32[256,16384]{1,0:T(8,128)}) fusion(bf16[16384,128]{1,0:T(8,128)(2,1)} %bitcast.39, bf16[16,256,128]{2,1,0:T(8,128)(2,1)} %get-tuple-element.110, s32[]{:T(128)} %get-tuple-element.100, pred[16384]{0:T(1024)(128)(4,1)S(1)} %broadcast_in_dim.37), kind=kOutput, calls=%fused_computation.23.clone.1 | convolution fusion | flops 1086324480 | bytes 21054976 | tf_op jit(solution)/shard_map/while/body/eval_jaxpr/dot_general | solution.py:10
  889.0 10.4 %fusion.23 = (f32[256]{0:T(256)S(1)}, f32[256,16384]{1,0:T(8,128)}) fusion(bf16[16384,128]{1,0:T(8,128)(2,1)} %bitcast.39, bf16[16,256,128]{2,1,0:T(8,128)(2,1)} %get-tuple-element.110, s32[]{:T(128)} %get-tuple-element.100, pred[16384]{0:T(1024)(128)(4,1)S(1)} %broadcast_in_dim.37), kind=kOutput, calls=%fused_computation.23.clone.1 | convolution fusion | flops 1086324480 | bytes 21054976 | tf_op jit(solution)/shard_map/while/body/eval_jaxpr/dot_general | solution.py:10
  925.0 10.4 %fusion.23 = (f32[256]{0:T(256)S(1)}, f32[256,16384]{1,0:T(8,128)}) fusion(bf16[16384,128]{1,0:T(8,128)(2,1)} %bitcast.39, bf16[16,256,128]{2,1,0:T(8,128)(2,1)} %get-tuple-element.110, s32[]{:T(128)} %get-tuple-element.100, pred[16384]{0:T(1024)(128)(4,1)S(1)} %broadcast_in_dim.37), kind=kOutput, calls=%fused_computation.23.clone.1 | convolution fusion | flops 1086324480 | bytes 21054976 | tf_op jit(solution)/shard_map/while/body/eval_jaxpr/dot_general | solution.py:10
  (168 shorter events, 375.7 us)
Async XLA Ops:
  0.0 13.9 %copy-start = (s32[256]{0:T(256)S(1)}, s32[256]{0:T(256)}, u32[]{:S(2)}) copy-start(s32[256]{0:T(256)} %param.9) | copy-start | bytes 3076
  7.1 6.7 copy-start.2
  7.1 368.8 %all-to-all-start = ((bf16[16,16,256,128]{3,2,1,0:T(8,128)(2,1)}), bf16[16,16,256,128]{3,2,1,0:T(8,128)(2,1)}, u32[]{:S(2)}, u32[]{:S(2)}) async-start(bf16[16,16,256,128]{3,2,1,0:T(8,128)(2,1)} %stack.2), calls=%async_computation | async-start | bytes 33554432 | tf_op jit(solution)/shard_map/all_to_all | solution.py:26
  385.6 18.6 %copy-start.1 = (bf16[64,256,128]{2,1,0:T(8,128)(2,1)S(1)}, bf16[64,256,128]{2,1,0:T(8,128)(2,1)}, u32[]{:S(2)}) copy-start(bf16[64,256,128]{2,1,0:T(8,128)(2,1)} %gather_fusion) | copy-start | bytes 12582916 | tf_op jit(solution)/shard_map/while
  421.5 18.6 %copy-start.1 = (bf16[64,256,128]{2,1,0:T(8,128)(2,1)S(1)}, bf16[64,256,128]{2,1,0:T(8,128)(2,1)}, u32[]{:S(2)}) copy-start(bf16[64,256,128]{2,1,0:T(8,128)(2,1)} %gather_fusion) | copy-start | bytes 12582916 | tf_op jit(solution)/shard_map/while
  457.5 18.6 %copy-start.1 = (bf16[64,256,128]{2,1,0:T(8,128)(2,1)S(1)}, bf16[64,256,128]{2,1,0:T(8,128)(2,1)}, u32[]{:S(2)}) copy-start(bf16[64,256,128]{2,1,0:T(8,128)(2,1)} %gather_fusion) | copy-start | bytes 12582916 | tf_op jit(solution)/shard_map/while
  493.5 18.6 %copy-start.1 = (bf16[64,256,128]{2,1,0:T(8,128)(2,1)S(1)}, bf16[64,256,128]{2,1,0:T(8,128)(2,1)}, u32[]{:S(2)}) copy-start(bf16[64,256,128]{2,1,0:T(8,128)(2,1)} %gather_fusion) | copy-start | bytes 12582916 | tf_op jit(solution)/shard_map/while
  529.4 18.6 %copy-start.1 = (bf16[64,256,128]{2,1,0:T(8,128)(2,1)S(1)}, bf16[64,256,128]{2,1,0:T(8,128)(2,1)}, u32[]{:S(2)}) copy-start(bf16[64,256,128]{2,1,0:T(8,128)(2,1)} %gather_fusion) | copy-start | bytes 12582916 | tf_op jit(solution)/shard_map/while
  565.4 18.6 %copy-start.1 = (bf16[64,256,128]{2,1,0:T(8,128)(2,1)S(1)}, bf16[64,256,128]{2,1,0:T(8,128)(2,1)}, u32[]{:S(2)}) copy-start(bf16[64,256,128]{2,1,0:T(8,128)(2,1)} %gather_fusion) | copy-start | bytes 12582916 | tf_op jit(solution)/shard_map/while
  601.3 18.6 %copy-start.1 = (bf16[64,256,128]{2,1,0:T(8,128)(2,1)S(1)}, bf16[64,256,128]{2,1,0:T(8,128)(2,1)}, u32[]{:S(2)}) copy-start(bf16[64,256,128]{2,1,0:T(8,128)(2,1)} %gather_fusion) | copy-start | bytes 12582916 | tf_op jit(solution)/shard_map/while
  637.3 18.6 %copy-start.1 = (bf16[64,256,128]{2,1,0:T(8,128)(2,1)S(1)}, bf16[64,256,128]{2,1,0:T(8,128)(2,1)}, u32[]{:S(2)}) copy-start(bf16[64,256,128]{2,1,0:T(8,128)(2,1)} %gather_fusion) | copy-start | bytes 12582916 | tf_op jit(solution)/shard_map/while
  673.2 18.6 %copy-start.1 = (bf16[64,256,128]{2,1,0:T(8,128)(2,1)S(1)}, bf16[64,256,128]{2,1,0:T(8,128)(2,1)}, u32[]{:S(2)}) copy-start(bf16[64,256,128]{2,1,0:T(8,128)(2,1)} %gather_fusion) | copy-start | bytes 12582916 | tf_op jit(solution)/shard_map/while
  709.2 18.6 %copy-start.1 = (bf16[64,256,128]{2,1,0:T(8,128)(2,1)S(1)}, bf16[64,256,128]{2,1,0:T(8,128)(2,1)}, u32[]{:S(2)}) copy-start(bf16[64,256,128]{2,1,0:T(8,128)(2,1)} %gather_fusion) | copy-start | bytes 12582916 | tf_op jit(solution)/shard_map/while
  745.2 18.6 %copy-start.1 = (bf16[64,256,128]{2,1,0:T(8,128)(2,1)S(1)}, bf16[64,256,128]{2,1,0:T(8,128)(2,1)}, u32[]{:S(2)}) copy-start(bf16[64,256,128]{2,1,0:T(8,128)(2,1)} %gather_fusion) | copy-start | bytes 12582916 | tf_op jit(solution)/shard_map/while
  781.1 18.6 %copy-start.1 = (bf16[64,256,128]{2,1,0:T(8,128)(2,1)S(1)}, bf16[64,256,128]{2,1,0:T(8,128)(2,1)}, u32[]{:S(2)}) copy-start(bf16[64,256,128]{2,1,0:T(8,128)(2,1)} %gather_fusion) | copy-start | bytes 12582916 | tf_op jit(solution)/shard_map/while
  817.1 18.6 %copy-start.1 = (bf16[64,256,128]{2,1,0:T(8,128)(2,1)S(1)}, bf16[64,256,128]{2,1,0:T(8,128)(2,1)}, u32[]{:S(2)}) copy-start(bf16[64,256,128]{2,1,0:T(8,128)(2,1)} %gather_fusion) | copy-start | bytes 12582916 | tf_op jit(solution)/shard_map/while
  853.0 18.6 %copy-start.1 = (bf16[64,256,128]{2,1,0:T(8,128)(2,1)S(1)}, bf16[64,256,128]{2,1,0:T(8,128)(2,1)}, u32[]{:S(2)}) copy-start(bf16[64,256,128]{2,1,0:T(8,128)(2,1)} %gather_fusion) | copy-start | bytes 12582916 | tf_op jit(solution)/shard_map/while
  889.0 18.6 %copy-start.1 = (bf16[64,256,128]{2,1,0:T(8,128)(2,1)S(1)}, bf16[64,256,128]{2,1,0:T(8,128)(2,1)}, u32[]{:S(2)}) copy-start(bf16[64,256,128]{2,1,0:T(8,128)(2,1)} %gather_fusion) | copy-start | bytes 12582916 | tf_op jit(solution)/shard_map/while
  925.0 18.6 %copy-start.1 = (bf16[64,256,128]{2,1,0:T(8,128)(2,1)S(1)}, bf16[64,256,128]{2,1,0:T(8,128)(2,1)}, u32[]{:S(2)}) copy-start(bf16[64,256,128]{2,1,0:T(8,128)(2,1)} %gather_fusion) | copy-start | bytes 12582916 | tf_op jit(solution)/shard_map/while
  951.2 1.0 copy-start.3
